TPU v7x, 256 devices: a whole 4x4x8 slice. The times are simulated.
256 devices in a mesh: row: 16 (over z, core), col: 4 (over x), seed: 4 (over y).
Axes of the slice: x: 4, y: 4, z: 8, core: 2. Of those that a mesh axis runs over, the one named last changes fastest.
Arguments:
- tiles: bfloat16 [16, 4, 384, 128, 128], P('row', 'col'), may hold values from -0.0390625 to 0.0390625
- tile_out: int32 [16, 4, 384], P('row', 'col'), may hold values from 0 to 15, as said below
- tile_in: int32 [16, 4, 384], P('row', 'col'), may hold values from 0 to 3
- tile_count: int32 [16, 4], P('row', 'col'), may hold values from 1 to 384, as said below
- out_degree: int32 [8192], P(('row', 'col')), may hold values from 1 to 8
- seed_ids: int32 [512, 16], P('seed'), may hold values from 0 to 8191
- prior: float32 [512, 8192], P('seed', ('row', 'col')), may hold values from -6 to 6
Outputs:
- risk: float32 [512, 8192], P('seed', ('row', 'col'))
Inputs may be any that keep to these rules, and one draw needn't show every extreme that they name: `tile_count`: occupied slots of a device come first; some device has all 384 occupied in every draw. `tile_out`: on every device the output blocks named by the occupied slots never fall from one slot to the next; several occupied slots of one device may name the same output block, and the same pair of blocks.
All inputs are finite; a program needn't handle non-finite values.
Results may differ from a plain program's by a relative error of at most 0.0041.
Values may be sent and summed in bfloat16 or wider, within the bound.
A program may use at most 64 MiB of HBM per device.

v0:
```python
import math
import jax
import jax.numpy as jnp
from jax import lax
from jax.sharding import PartitionSpec as P

ITERATIONS = 2
damping = 0.85


def products(blocks, tiles_here, out_ids, in_ids, first_slot, end_slot, base_block, block_total):
    slot_total = tiles_here.shape[0]
    group_size = math.gcd(slot_total, 32)
    sets_here = blocks.shape[1]
    block_edge = tiles_here.shape[2]
    offsets = jnp.arange(group_size, dtype=jnp.int32)
    first_group = first_slot // group_size
    end_group = (end_slot + group_size - 1) // group_size

    def advance(group_index, panel_sum):
        slot_start = group_index * group_size
        tile_block = lax.dynamic_slice_in_dim(tiles_here, slot_start, group_size, 0)
        targets = lax.dynamic_slice_in_dim(out_ids, slot_start, group_size, 0) - base_block
        sources = lax.dynamic_slice_in_dim(in_ids, slot_start, group_size, 0)
        gathered = jnp.take(blocks, sources, axis=0)
        product = jnp.einsum(
            "gsk,gkj->gsj", gathered, tile_block, preferred_element_type=jnp.float32
        )
        slot_here = slot_start + offsets
        valid_mask = ((slot_here >= first_slot) & (slot_here < end_slot)).astype(jnp.float32)
        targets = jnp.clip(targets, 0, block_total - 1)
        return panel_sum.at[targets].add(product * valid_mask[:, None, None])

    zero_panel = jnp.zeros((block_total, sets_here, block_edge), jnp.float32)
    return lax.fori_loop(first_group, end_group, advance, zero_panel)


def local(tiles, tile_out, tile_in, tile_count, out_degree, seed_ids, prior):
    tiles_here = tiles[0, 0]
    out_ids = tile_out[0, 0]
    in_ids = tile_in[0, 0]
    occupied = tile_count[0, 0]
    row_devices = lax.axis_size("row")
    col_devices = lax.axis_size("col")
    sets_here, owned_count = prior.shape
    block_edge = tiles_here.shape[1]
    owned_blocks = owned_count // block_edge
    out_blocks = row_devices * owned_blocks
    own_start = (lax.axis_index("row") * col_devices + lax.axis_index("col")) * owned_count
    local_ids = seed_ids - own_start
    positions = jnp.arange(owned_count, dtype=jnp.int32)
    restart_rows = jnp.sum(
        (local_ids[:, :, None] == positions[None, None, :]).astype(jnp.float32), axis=1
    )
    restart = restart_rows.reshape(sets_here, owned_blocks, block_edge).transpose(1, 0, 2)
    degree = out_degree.astype(jnp.float32).reshape(owned_blocks, 1, block_edge)
    risk_now = prior.reshape(sets_here, owned_blocks, block_edge).transpose(1, 0, 2)
    for round_index in range(ITERATIONS):
        scaled = (risk_now / degree).astype(jnp.bfloat16)
        blocks = lax.all_gather(scaled, "col", axis=0, tiled=True)
        partial_value = products(blocks, tiles_here, out_ids, in_ids, 0, occupied, 0, out_blocks)
        incoming = lax.psum_scatter(partial_value, "row", scatter_dimension=0, tiled=True)
        risk_now = (1.0 - damping) * restart + damping * incoming
    return risk_now.transpose(1, 0, 2).reshape(sets_here, owned_count)


def solution(mesh):
    placed = (
        P("row", "col", None, None, None),
        P("row", "col", None),
        P("row", "col", None),
        P("row", "col"),
        P(("row", "col")),
        P("seed", None),
        P("seed", ("row", "col")),
    )
    return jax.shard_map(
        local, mesh=mesh, in_specs=placed, out_specs=P("seed", ("row", "col")), check_vma=False
    )
```

profile of v0, /device:TPU:4, one launch (start us, length us, event | category | flops | bytes accessed | tf_op | source)
XLA Modules:
  0.0 331.0 jit_solution(5670135569856032543)
XLA Ops:
  8.7 12.1 %all-gather = bf16[512,128]{1,0:T(8,128)(2,1)S(1)} all-gather(bf16[128,128]{1,0:T(8,128)(2,1)S(1)} %divide_convert_fusion), channel_id=2, replica_groups=mesh['row'=16,'col'=4,'seed'=4] {'col'}, dimensions={0}, use_global_device_ids=true | all-gather | bytes 163840 | tf_op jit(solution)/shard_map/all_gather | solution.py:60
  22.4 21.6 %while.22 = (s32[]{:T(128)}, f32[16,128,128]{2,1,0:T(8,128)S(1)}, s32[]{:T(128)}, s32[384]{0:T(512)S(1)}, s32[384]{0:T(512)S(1)}, /*index=5*/bf16[4,128,128]{2,1...) while((s32[]{:T(128)}, f32[16,128,128]{2,1,0:T(8,128)S(1)}, ...), condition=%wide.region_3.5_spmd.clone, body=%wide.region_1.4_spmd.clone.sunk | while | flops 135792096 | bytes 12588407 | solution.py:35
  23.1 1.7 gather_fusion
  24.8 2.0 convolution_multiply_fusion.4
  26.9 2.7 scatter_fusion
  30.4 1.7 gather_fusion
  32.0 2.0 convolution_multiply_fusion.4
  34.1 2.7 scatter_fusion
  37.6 1.7 gather_fusion
  39.2 2.0 convolution_multiply_fusion.4
  41.4 2.7 scatter_fusion
  45.6 123.5 %reduce-scatter.3.cloned.1.call-done = f32[1,128,128]{2,1,0:T(8,128)} async-done(((f32[16,128,128]{2,1,0:T(8,128)}), f32[1,128,128]{2,1,0:T(8,128)}) %reduce-scatter.3.cloned.1.call-update) | async-done | bytes 65552 | tf_op jit(solution)/shard_map/reduce_scatter | solution.py:62
  169.9 10.8 %all_gather.7 = bf16[4,128,128]{2,1,0:T(8,128)(2,1)S(1)} all-gather(bf16[1,128,128]{2,1,0:T(8,128)(2,1)S(1)} %fusion.17), channel_id=1, replica_groups=mesh['row'=16,'col'=4,'seed'=4] {'col'}, dimensions={0}, use_global_device_ids=true | all-gather | bytes 163840 | tf_op jit(solution)/shard_map/all_gather | solution.py:60
  180.8 21.6 %while.23 = (s32[]{:T(128)}, f32[16,128,128]{2,1,0:T(8,128)S(1)}, s32[]{:T(128)}, s32[384]{0:T(512)S(1)}, s32[384]{0:T(512)S(1)}, /*index=5*/bf16[4,128,128]{2,1...) while((s32[]{:T(128)}, f32[16,128,128]{2,1,0:T(8,128)S(1)}, ...), condition=%wide.region_7.9_spmd.clone, body=%wide.region_5.8_spmd.clone.sunk | while | flops 135792096 | bytes 12588407 | solution.py:35
  181.6 1.7 gather_fusion.1
  183.3 2.0 convolution_multiply_fusion.5
  185.4 2.7 scatter_fusion.1
  188.8 1.7 gather_fusion.1
  190.5 2.0 convolution_multiply_fusion.5
  192.6 2.7 scatter_fusion.1
  196.0 1.7 gather_fusion.1
  197.7 2.0 convolution_multiply_fusion.5
  199.8 2.7 scatter_fusion.1
  203.5 119.2 %reduce-scatter.5.cloned.1.call-done = f32[1,128,128]{2,1,0:T(8,128)} async-done(((f32[16,128,128]{2,1,0:T(8,128)}), f32[1,128,128]{2,1,0:T(8,128)}) %reduce-scatter.5.cloned.1.call-update) | async-done | bytes 65552 | tf_op jit(solution)/shard_map/reduce_scatter | solution.py:62
  (39 shorter events, 12.9 us)
Async XLA Ops:
  6.5 162.5 %reduce-scatter.3.cloned.1.call-start = ((), (), s32[]{:S(2)}) async-start(), calls=%async_computation.2 | async-start | bytes 1114112 | tf_op jit(solution)/shard_map/reduce_scatter | solution.py:62
  22.4 22.7 %copy-start.2 = (s32[128,16]{0,1:T(8,128)S(1)}, s32[128,16]{0,1:T(8,128)}, u32[]{:S(2)}) copy-start(s32[128,16]{0,1:T(8,128)} %param.18) | copy-start | bytes 24580
  44.0 1.0 copy-start.1
  45.0 277.7 %reduce-scatter.5.cloned.1.call-start = ((), (), s32[]{:S(2)}) async-start(), calls=%async_computation.3 | async-start | bytes 1114112 | tf_op jit(solution)/shard_map/reduce_scatter | solution.py:62
  202.5 1.0 copy-start
Sparse Core Ops, SparseCore 0:
  45.2 123.8 reduce-scatter.2
  203.6 119.0 reduce-scatter.4
where the time goes:
time: 332 us; the launch traced here: 331 us
  waiting for transfers between devices  243 us (73%)
  other arithmetic  26.5 us (8%)
  blocking collectives  22.9 us (7%)
  between operations  14.2 us (4%)
  local copies, waits for them, and re-layouts  12.3 us (4%)
  matrix products  12.2 us (4%)
    reduce_scatter x2, waiting for transfers between devices, local(): lax.psum_scatter(partial_value, 'row', scatter_dimension=0, tiled=True)  243 us
    all_gather x2, blocking collectives, local(): blocks = lax.all_gather(scaled, 'col', axis=0, tiled=True)  22.9 us
    scatter-add x6, other arithmetic, advance(): return panel_sum.at[targets].add(product * valid_mask[:, None, None])  15.9 us
    dot_general x6, matrix products, advance(): jnp.einsum('gsk,gkj->gsj', gathered, tile_block, preferred_element_type=j...  12.2 us
    gather x6, local copies, waits for them, and re-layouts, advance(): gathered = jnp.take(blocks, sources, axis=0)  10 us
  transfers between devices with their start and end apart: 2, of which 2 were waited for; matrix products, arithmetic and copies ran while one was open for 0% of the time, Pallas kernels for 0%

commit v1 on v0

--- a/solution.py
+++ b/solution.py
@@ -57,7 +57,9 @@
     risk_now = prior.reshape(sets_here, owned_blocks, block_edge).transpose(1, 0, 2)
     for round_index in range(ITERATIONS):
         scaled = (risk_now / degree).astype(jnp.bfloat16)
-        blocks = lax.all_gather(scaled, "col", axis=0, tiled=True)
+        blocks = jnp.concatenate(
+            lax.all_to_all(jnp.stack([scaled] * lax.axis_size("col")), "col", 0, 0), axis=0
+        )
         partial_value = products(blocks, tiles_here, out_ids, in_ids, 0, occupied, 0, out_blocks)
         incoming = lax.psum_scatter(partial_value, "row", scatter_dimension=0, tiled=True)
         risk_now = (1.0 - damping) * restart + damping * incoming

time: 332 us -> 327 us (0.985)
  blocking collectives: 22.9 us -> 0 us
  starting transfers between devices: 0.04 us -> 10.3 us
  waiting for transfers between devices: 243 us -> 249 us
    all_gather x2 -> x0, blocking collectives: 22.9 us -> none  [local(): blocks = lax.all_gather(scaled, 'col', axis=0, tiled=True)]
    all_to_all x0 -> x2, starting transfers between devices: none -> 10.3 us  [local(): lax.all_to_all(jnp.stack([scaled] * lax.axis_size('col')), 'col', 0, 0)]
    all_to_all x0 -> x2, waiting for transfers between devices: none -> 4.46 us  [local(): lax.all_to_all(jnp.stack([scaled] * lax.axis_size('col')), 'col', 0, 0)]
  transfers between devices with their start and end apart: 2 -> 4, of which waited for: 2 -> 4; matrix products, arithmetic and copies ran while one was open for 0% -> 1% of each run, Pallas kernels for 0% -> 0%
where the time goes in v1:
time: 327 us; the launch traced here: 326 us
  waiting for transfers between devices  249 us (76%)
  other arithmetic  26.5 us (8%)
  between operations  14.2 us (4%)
  local copies, waits for them, and re-layouts  13.6 us (4%)
  matrix products  12.2 us (4%)
  starting transfers between devices  10.3 us (3%)
    reduce_scatter x2, waiting for transfers between devices, local(): lax.psum_scatter(partial_value, 'row', scatter_dimension=0, tiled=True)  244 us
    scatter-add x6, other arithmetic, advance(): return panel_sum.at[targets].add(product * valid_mask[:, None, None])  15.9 us
    dot_general x6, matrix products, advance(): jnp.einsum('gsk,gkj->gsj', gathered, tile_block, preferred_element_type=j...  12.2 us
    all_to_all x2, starting transfers between devices, local(): lax.all_to_all(jnp.stack([scaled] * lax.axis_size('col')), 'col', 0, 0)  10.3 us
    gather x6, local copies, waits for them, and re-layouts, advance(): gathered = jnp.take(blocks, sources, axis=0)  10 us
  transfers between devices with their start and end apart: 4, of which 4 were waited for; matrix products, arithmetic and copies ran while one was open for 1% of the time, Pallas kernels for 0%

profile of v1, /device:TPU:4, one launch (start us, length us, event | category | flops | bytes accessed | tf_op | source)
XLA Modules:
  0.0 325.9 jit_solution(8475140654988433917)
XLA Ops:
  8.7 5.5 %all-to-all-start = ((bf16[4,1,128,128]{3,2,1,0:T(8,128)(2,1)}), bf16[4,1,128,128]{3,2,1,0:T(8,128)(2,1)S(1)}, u32[]{:S(2)}, u32[]{:S(2)}) async-start(bf16[4,1,128,128]{3,2,1,0:T(8,128)(2,1)} %stack.4), calls=%async_computation | async-start | bytes 262144 | tf_op jit(solution)/shard_map/all_to_all | solution.py:61
  17.6 21.6 %while.22 = (s32[]{:T(128)}, f32[16,128,128]{2,1,0:T(8,128)S(1)}, s32[]{:T(128)}, s32[384]{0:T(512)S(1)}, s32[384]{0:T(512)S(1)}, /*index=5*/bf16[4,128,128]{2,1...) while((s32[]{:T(128)}, f32[16,128,128]{2,1,0:T(8,128)S(1)}, ...), condition=%wide.region_3.5_spmd.clone, body=%wide.region_1.4_spmd.clone.sunk | while | flops 135792096 | bytes 12588407 | solution.py:35
  18.4 1.7 gather_fusion
  20.0 2.0 convolution_multiply_fusion.4
  22.1 2.7 scatter_fusion
  25.6 1.7 gather_fusion
  27.2 2.0 convolution_multiply_fusion.4
  29.4 2.7 scatter_fusion
  32.8 1.7 gather_fusion
  34.5 2.0 convolution_multiply_fusion.4
  36.6 2.7 scatter_fusion
  40.8 124.2 %reduce-scatter.3.cloned.1.call-done = f32[1,128,128]{2,1,0:T(8,128)} async-done(((f32[16,128,128]{2,1,0:T(8,128)}), f32[1,128,128]{2,1,0:T(8,128)}) %reduce-scatter.3.cloned.1.call-update) | async-done | bytes 65552 | tf_op jit(solution)/shard_map/reduce_scatter | solution.py:64
  166.5 4.8 %all-to-all-start.1 = ((bf16[4,1,128,128]{3,2,1,0:T(8,128)(2,1)}), bf16[4,1,128,128]{3,2,1,0:T(8,128)(2,1)S(1)}, u32[]{:S(2)}, u32[]{:S(2)}) async-start(bf16[4,1,128,128]{3,2,1,0:T(8,128)(2,1)} %stack.5), calls=%async_computation.2 | async-start | bytes 262144 | tf_op jit(solution)/shard_map/all_to_all | solution.py:61
  171.3 3.3 %all-to-all-done.1 = bf16[4,1,128,128]{3,2,1,0:T(8,128)(2,1)S(1)} async-done(((bf16[4,1,128,128]{3,2,1,0:T(8,128)(2,1)}), bf16[4,1,128,128]{3,2,1,0:T(8,128)(2,1)S(1)}, u32[]{:S(2)}, u32[]{:S(2)}) %all-to-all-start.1) | async-done | bytes 131104 | tf_op jit(solution)/shard_map/all_to_all | solution.py:61
  174.6 21.6 %while.23 = (s32[]{:T(128)}, f32[16,128,128]{2,1,0:T(8,128)S(1)}, s32[]{:T(128)}, s32[384]{0:T(512)S(1)}, s32[384]{0:T(512)S(1)}, /*index=5*/bf16[4,128,128]{2,1...) while((s32[]{:T(128)}, f32[16,128,128]{2,1,0:T(8,128)S(1)}, ...), condition=%wide.region_7.9_spmd.clone, body=%wide.region_5.8_spmd.clone.sunk | while | flops 135792096 | bytes 12588407 | solution.py:35
  175.4 1.7 gather_fusion.1
  177.1 2.0 convolution_multiply_fusion.5
  179.2 2.7 scatter_fusion.1
  182.6 1.7 gather_fusion.1
  184.3 2.0 convolution_multiply_fusion.5
  186.4 2.7 scatter_fusion.1
  191.5 2.0 convolution_multiply_fusion.5
  193.6 2.7 scatter_fusion.1
  197.3 120.2 %reduce-scatter.5.cloned.1.call-done = f32[1,128,128]{2,1,0:T(8,128)} async-done(((f32[16,128,128]{2,1,0:T(8,128)}), f32[1,128,128]{2,1,0:T(8,128)}) %reduce-scatter.5.cloned.1.call-update) | async-done | bytes 65552 | tf_op jit(solution)/shard_map/reduce_scatter | solution.py:64
  (43 shorter events, 17.0 us)
Async XLA Ops:
  8.7 8.8 %all-to-all-start = ((bf16[4,1,128,128]{3,2,1,0:T(8,128)(2,1)}), bf16[4,1,128,128]{3,2,1,0:T(8,128)(2,1)S(1)}, u32[]{:S(2)}, u32[]{:S(2)}) async-start(bf16[4,1,128,128]{3,2,1,0:T(8,128)(2,1)} %stack.4), calls=%async_computation | async-start | bytes 262144 | tf_op jit(solution)/shard_map/all_to_all | solution.py:61
  14.2 150.7 %reduce-scatter.3.cloned.1.call-start = ((), (), s32[]{:S(2)}) async-start(), calls=%async_computation.4 | async-start | bytes 1114112 | tf_op jit(solution)/shard_map/reduce_scatter | solution.py:64
  17.6 22.7 %copy-start.2 = (s32[128,16]{0,1:T(8,128)S(1)}, s32[128,16]{0,1:T(8,128)}, u32[]{:S(2)}) copy-start(s32[128,16]{0,1:T(8,128)} %param.18) | copy-start | bytes 24580
  39.2 1.0 copy-start.1
  166.5 8.1 %all-to-all-start.1 = ((bf16[4,1,128,128]{3,2,1,0:T(8,128)(2,1)}), bf16[4,1,128,128]{3,2,1,0:T(8,128)(2,1)S(1)}, u32[]{:S(2)}, u32[]{:S(2)}) async-start(bf16[4,1,128,128]{3,2,1,0:T(8,128)(2,1)} %stack.5), calls=%async_computation.2 | async-start | bytes 262144 | tf_op jit(solution)/shard_map/all_to_all | solution.py:61
  171.2 146.3 %reduce-scatter.5.cloned.1.call-start = ((), (), s32[]{:S(2)}) async-start(), calls=%async_computation.5 | async-start | bytes 1114112 | tf_op jit(solution)/shard_map/reduce_scatter | solution.py:64
  196.3 1.0 copy-start
Sparse Core Ops, SparseCore 0:
  40.4 124.5 reduce-scatter.2
  197.4 120.0 reduce-scatter.4
